TPU v7x, 512 devices: a whole 4x4x16 slice. The times are simulated.
512 devices in a mesh: section: 2 (over y_hi), wide: 64 (over z, y_lo, core), narrow: 4 (over x).
Axes of the slice: x: 4, y: 4 (y_hi: 2, y_lo: 2; y = y_hi * 2 + y_lo), z: 16, core: 2. Of those that a mesh axis runs over, the one named last changes fastest.
Arguments:
- token_shard: int32 [16384, 1], P(('section', 'wide')), may hold values from 0 to 127; in each aligned block of 128 rows (0 to 127, 128 to 255, ...) at most 2 rows name the same one
- token_row: int32 [16384], P(('section', 'wide')), may hold values from 0 to 511
- table: bfloat16 [65536, 8192], P(('section', 'wide'), 'narrow'), may hold values from -51 to 51
- gain: float32 [8192], P('narrow'), may hold values from 0.1 to 1.9
- key_value_weight: bfloat16 [2048, 8192], P(('section', 'wide'), 'narrow'), may hold values from -0.0625 to 0.0625
- kv_target: bfloat16 [16384, 2048], P(('section', 'wide'), 'narrow'), may hold values from -6 to 6
Outputs:
- table_grad: bfloat16 [65536, 8192], P(('section', 'wide'), 'narrow')
Inputs may be any that keep to these rules, and one draw needn't show every extreme that they name: `token_shard`: among the rows of one device, no value is named by more than 2 rows.
All inputs are finite; a program needn't handle non-finite values.
Results may differ from a plain program's by a relative error of at most 0.0056.
Values may be sent and summed in bfloat16 or wider, within the bound.
A program may use at most 64 MiB of HBM per device.

v0:
```python
import jax
import jax.numpy as jnp
from jax import lax
from jax.sharding import PartitionSpec as P

D = 8192


EPSILON = 1e-05


def contract_last(left, right):
    return lax.dot_general(
        left, right, (((1,), (1,)), ((), ())), preferred_element_type=jnp.float32
    )


def on_device(token_shard, token_row, table, gain, key_value_weight, kv_target):
    tokens_here = token_row.shape[0]
    owners = lax.axis_size(("section", "wide"))
    slot_count = 2 * tokens_here // owners
    width_here = table.shape[1]
    shard_of = token_shard[:, 0]
    membership = (shard_of[:, None] == jnp.arange(owners, dtype=jnp.int32)[None, :]).astype(
        jnp.int32
    )
    ranking = jnp.sum((jnp.cumsum(membership, axis=0) - 1) * membership, axis=1)
    position = shard_of * slot_count + ranking
    requests = (
        jnp.full((owners * slot_count,), -1, jnp.int32)
        .at[position]
        .set(token_row)
        .reshape(owners, slot_count)
    )
    holder = (
        jnp.full((owners * slot_count,), -1, jnp.int32)
        .at[position]
        .set(jnp.arange(tokens_here, dtype=jnp.int32))
    )
    wanted = lax.all_to_all(requests, ("section", "wide"), split_axis=0, concat_axis=0, tiled=True)
    present = wanted >= 0
    picked = jnp.take(table, jnp.where(present, wanted, 0), axis=0)
    returned = lax.all_to_all(
        jnp.where(present[..., None], picked, jnp.zeros((), table.dtype)),
        ("section", "wide"),
        split_axis=0,
        concat_axis=0,
        tiled=True,
    )
    hidden = jnp.take(returned.reshape(owners * slot_count, width_here), position, axis=0)
    rows_float = hidden.astype(jnp.float32)
    mean_square = lax.psum(jnp.sum(rows_float * rows_float, axis=1), "narrow") / D
    row_scale = lax.rsqrt(mean_square + EPSILON)
    normed = (rows_float * row_scale[:, None] * gain[None, :]).astype(jnp.bfloat16)
    weight_full = lax.all_gather(key_value_weight, ("section", "wide"), axis=0, tiled=True)
    partial_value = contract_last(normed, weight_full)
    projected = lax.psum_scatter(partial_value, "narrow", scatter_dimension=1, tiled=True)
    residual = (projected - kv_target.astype(jnp.float32)).astype(jnp.bfloat16)
    residual_full = lax.all_gather(residual, "narrow", axis=1, tiled=True)
    back_rows = jnp.dot(residual_full, weight_full, preferred_element_type=jnp.float32)
    weighted = back_rows * gain[None, :]
    inner_sum = lax.psum(jnp.sum(weighted * rows_float, axis=1), "narrow")
    grad_rows = (
        row_scale[:, None] * weighted - rows_float * (row_scale**3 * inner_sum / D)[:, None]
    ).astype(jnp.bfloat16)
    occupied = holder >= 0
    outgoing = jnp.where(
        occupied[:, None],
        jnp.take(grad_rows, jnp.where(occupied, holder, 0), axis=0),
        jnp.zeros((), jnp.bfloat16),
    )
    incoming = lax.all_to_all(
        outgoing.reshape(owners, slot_count, width_here),
        ("section", "wide"),
        split_axis=0,
        concat_axis=0,
        tiled=True,
    )
    vocab_rows = table.shape[0]
    matches = (
        wanted.reshape(1, owners * slot_count) == jnp.arange(vocab_rows, dtype=jnp.int32)[:, None]
    ).astype(jnp.bfloat16)
    table_grad = jnp.dot(
        matches,
        incoming.reshape(owners * slot_count, width_here),
        preferred_element_type=jnp.float32,
    )
    return table_grad.astype(jnp.bfloat16)


def solution(mesh):
    return jax.shard_map(
        on_device,
        mesh=mesh,
        in_specs=(
            P(("section", "wide"), None),
            P(("section", "wide")),
            P(("section", "wide"), "narrow"),
            P("narrow"),
            P(("section", "wide"), "narrow"),
            P(("section", "wide"), "narrow"),
        ),
        out_specs=P(("section", "wide"), "narrow"),
        check_vma=False,
    )
```

profile of v0, /device:TPU:1, one launch (start us, length us, event | category | flops | bytes accessed | tf_op | source)
XLA Modules:
  0.0 417.6 jit_solution(1082262638751350529)
XLA Ops:
  6.5 0.0 copy-start
  6.5 0.0 all-gather.2.cloned.1.call-start
  6.5 0.7 all-gather.2.cloned.1.call-update
  7.3 0.7 fusion.11
  8.0 0.2 reduce_window_sum.11
  8.2 0.8 select_reduce_fusion
  9.0 0.7 and_bitcast_fusion
  9.7 1.1 scatter_custom_fusion
  10.8 0.1 all_to_all.16
  10.9 35.0 %all_to_all.25 = s32[128,1,2]{2,1,0:T(1,128)S(1)} all-to-all(s32[128,1,2]{2,1,0:T(1,128)S(1)} %bitcast.20), channel_id=1, replica_groups=mesh['section'=2,'wide'=64,'narrow'=4] {'section','wide'}, dimensions={0} | all-to-all | bytes 2048 | tf_op jit(solution)/shard_map/all_to_all | solution.py:40
  45.9 0.1 reshape.81
  46.1 0.0 copy-done
  46.1 1.4 gather_fusion
  47.5 0.0 copy-start.3
  47.5 1.5 reshape.80
  49.0 3.2 broadcast_select_fusion.1
  52.3 7.8 %all-to-all-start.1 = ((bf16[128,2,2048]{2,1,0:T(2,128)(2,1)}), bf16[128,2,2048]{2,1,0:T(2,128)(2,1)}, u32[]{:S(2)}, u32[]{:S(2)}) async-start(bf16[128,2,2048]{2,1,0:T(2,128)(2,1)} %broadcast_select_fusion.1), calls=%async_computation.1 | async-start | bytes 2097152 | tf_op jit(solution)/shard_map/all_to_all | solution.py:43
  60.1 0.0 reduce-scatter.2.cloned.1.call-start
  60.2 58.5 %all-to-all-done.1 = bf16[128,2,2048]{2,1,0:T(2,128)(2,1)} async-done(((bf16[128,2,2048]{2,1,0:T(2,128)(2,1)}), bf16[128,2,2048]{2,1,0:T(2,128)(2,1)}, u32[]{:S(2)}, u32[]{:S(2)}) %all-to-all-start.1) | async-done | bytes 1048608 | tf_op jit(solution)/shard_map/all_to_all | solution.py:43
  118.7 1.5 reshape.77
  120.1 0.0 copy-start.2
  120.2 1.8 gather_fusion.1
  121.9 0.0 copy-start.1
  121.9 1.4 fusion
  123.3 8.5 %psum.14 = f32[128]{0:T(128)S(1)} all-reduce(f32[128]{0:T(128)S(1)} %fusion), channel_id=1, replica_groups=mesh['section'=2,'wide'=64,'narrow'=4] {'narrow'}, use_global_device_ids=true, to_apply=%region_5.6 | all-reduce | flops 128 | bytes 1024 | tf_op jit(solution)/shard_map/psum | solution.py:52
  131.8 129.1 %all-gather.2.cloned.1.call-done = bf16[2048,2048]{1,0:T(8,128)(2,1)} async-done(((bf16[16,2048]{1,0:T(8,128)(2,1)}), bf16[2048,2048]{1,0:T(8,128)(2,1)}) %all-gather.2.cloned.1.call-update) | async-done | bytes 8388624 | tf_op jit(solution)/shard_map/all_gather | solution.py:55
  260.9 0.0 copy-done.3
  260.9 7.4 %fusion.6 = f32[128,2048]{1,0:T(8,128)} fusion(bf16[2048,2048]{1,0:T(8,128)(2,1)} %all-gather.2.cloned.1.call-done, f32[2048]{0:T(1024)S(1)} %copy-done.3, f32[128]{0:T(128)S(1)} %add_rsqrt_fusion, bf16[128,2048]{1,0:T(8,128)(2,1)} %gather_fusion.1, pred[128]{0:T(512)(128)(4,1)S(1)} %get-tuple-element.7), kind=kOutput, calls=%fused_computation.21 | convolution fusion | flops 1075052544 | bytes 9970304 | tf_op jit(solution)/shard_map/dot_general | solution.py:13
  268.4 0.0 reduce-scatter.2.cloned.1.call-update
  268.4 1.0 scatter_custom_fusion.1
  269.4 0.2 broadcast_in_dim.71
  269.6 0.2 broadcast_in_dim.73
  269.7 26.5 %reduce-scatter.2.cloned.1.call-done = f32[128,512]{1,0:T(8,128)} async-done(((f32[128,2048]{1,0:T(8,128)}), f32[128,512]{1,0:T(8,128)}) %reduce-scatter.2.cloned.1.call-update) | async-done | bytes 262160 | tf_op jit(solution)/shard_map/reduce_scatter | solution.py:57
  296.3 0.0 copy-done.2
  296.3 1.0 subtract_convert_fusion
  297.3 10.7 %all_gather.7 = bf16[128,2048]{1,0:T(8,128)(2,1)S(1)} all-gather(bf16[128,512]{1,0:T(8,128)(2,1)S(1)} %subtract_convert_fusion), channel_id=1, replica_groups=mesh['section'=2,'wide'=64,'narrow'=4] {'narrow'}, dimensions={1}, use_global_device_ids=true | all-gather | bytes 655360 | tf_op jit(solution)/shard_map/all_gather | solution.py:59
  307.9 0.0 copy-done.1
  307.9 5.7 %fusion.3 = (f32[128]{0:T(128)S(1)}, f32[128,2048]{1,0:T(8,128)}) fusion(bf16[128,2048]{1,0:T(8,128)(2,1)S(1)} %copy-done.1, pred[128]{0:T(512)(128)(4,1)S(1)} %get-tuple-element.7, f32[2048]{0:T(1024)S(1)} %copy-done.3, bf16[128,2048]{1,0:T(8,128)(2,1)S(1)} %all_gather.7, bf16[2048,2048]{1,0:T(8,128)(2,1)} %all-gather.2.cloned.1.call-done), kind=kOutput, calls=%fused_computation.18 | convolution fusion | flops 1075052416 | bytes 10494592 | tf_op jit(solution)/shard_map/dot_general | solution.py:60
  313.7 6.0 %psum.15 = f32[128]{0:T(128)S(1)} all-reduce(f32[128]{0:T(128)S(1)} %get-tuple-element.12), channel_id=1, replica_groups=mesh['section'=2,'wide'=64,'narrow'=4] {'narrow'}, use_global_device_ids=true, to_apply=%region_8.9 | all-reduce | flops 128 | bytes 1024 | tf_op jit(solution)/shard_map/psum | solution.py:62
  319.7 1.5 fusion.5
  321.2 2.3 gather_fusion.2
  323.5 1.7 gather.17
  325.3 2.4 broadcast_select_fusion.3
  327.7 23.3 %all-to-all-start.2 = ((bf16[128,2,2048]{2,1,0:T(2,128)(2,1)}), bf16[128,2,2048]{2,1,0:T(2,128)(2,1)S(1)}, u32[]{:S(2)}, u32[]{:S(2)}) async-start(bf16[128,2,2048]{2,1,0:T(2,128)(2,1)} %broadcast_select_fusion.3), calls=%async_computation.3 | async-start | bytes 2097152 | tf_op jit(solution)/shard_map/all_to_all | solution.py:72
  351.0 0.6 broadcast.120
  351.5 0.8 reduce.3
  352.4 0.1 eq.34
  352.5 53.7 %all-to-all-done.2 = bf16[128,2,2048]{2,1,0:T(2,128)(2,1)S(1)} async-done(((bf16[128,2,2048]{2,1,0:T(2,128)(2,1)}), bf16[128,2,2048]{2,1,0:T(2,128)(2,1)S(1)}, u32[]{:S(2)}, u32[]{:S(2)}) %all-to-all-start.2) | async-done | bytes 1048608 | tf_op jit(solution)/shard_map/all_to_all | solution.py:72
  406.3 1.2 reshape.78
  407.5 3.3 convolution_convert_fusion
  (9 shorter events, 0.1 us)
Async XLA Ops:
  6.5 39.6 %copy-start = (bf16[512,2048]{1,0:T(8,128)(2,1)S(1)}, bf16[512,2048]{1,0:T(8,128)(2,1)}, u32[]{:S(2)}) copy-start(bf16[512,2048]{1,0:T(8,128)(2,1)} %param.8) | copy-start | bytes 6291460
  6.5 254.4 %all-gather.2.cloned.1.call-start = ((), (), s32[]{:S(2)}) async-start(), calls=%async_computation.4 | async-start | bytes 8454144 | tf_op jit(solution)/shard_map/all_gather | solution.py:55
  47.5 213.5 %copy-start.3 = (f32[2048]{0:T(1024)S(1)}, f32[2048]{0:T(1024)}, u32[]{:S(2)}) copy-start(f32[2048]{0:T(1024)} %param.9) | copy-start | bytes 24580
  52.3 66.4 %all-to-all-start.1 = ((bf16[128,2,2048]{2,1,0:T(2,128)(2,1)}), bf16[128,2,2048]{2,1,0:T(2,128)(2,1)}, u32[]{:S(2)}, u32[]{:S(2)}) async-start(bf16[128,2,2048]{2,1,0:T(2,128)(2,1)} %broadcast_select_fusion.1), calls=%async_computation.1 | async-start | bytes 2097152 | tf_op jit(solution)/shard_map/all_to_all | solution.py:43
  60.1 236.1 %reduce-scatter.2.cloned.1.call-start = ((), (), s32[]{:S(2)}) async-start(), calls=%async_computation.5 | async-start | bytes 1310720 | tf_op jit(solution)/shard_map/reduce_scatter | solution.py:57
  120.1 176.1 %copy-start.2 = (bf16[128,512]{1,0:T(8,128)(2,1)S(1)}, bf16[128,512]{1,0:T(8,128)(2,1)}, u32[]{:S(2)}) copy-start(bf16[128,512]{1,0:T(8,128)(2,1)} %param.11) | copy-start | bytes 393220
  121.9 186.0 %copy-start.1 = (bf16[128,2048]{1,0:T(8,128)(2,1)S(1)}, bf16[128,2048]{1,0:T(8,128)(2,1)}, u32[]{:S(2)}) copy-start(bf16[128,2048]{1,0:T(8,128)(2,1)} %gather_fusion.1) | copy-start | bytes 1572868
  327.7 78.6 %all-to-all-start.2 = ((bf16[128,2,2048]{2,1,0:T(2,128)(2,1)}), bf16[128,2,2048]{2,1,0:T(2,128)(2,1)S(1)}, u32[]{:S(2)}, u32[]{:S(2)}) async-start(bf16[128,2,2048]{2,1,0:T(2,128)(2,1)} %broadcast_select_fusion.3), calls=%async_computation.3 | async-start | bytes 2097152 | tf_op jit(solution)/shard_map/all_to_all | solution.py:72
Sparse Core Ops, SparseCore 0:
  9.5 251.3 all-gather.1
  268.5 27.6 reduce-scatter.1
where the time goes:
time: 418 us
  waiting for transfers between devices  269 us (64%)
  blocking collectives  60.2 us (14%)
  starting transfers between devices  31.1 us (7%)
  matrix products  16.4 us (4%)
  local copies, waits for them, and re-layouts  14.8 us (4%)
  between operations  13.6 us (3%)
  other arithmetic  12.9 us (3%)
    all_gather x1, waiting for transfers between devices, on_device(): lax.all_gather(key_value_weight, ('section', 'wide'), axis=0, tiled=True)  129 us
    all_to_all x1, waiting for transfers between devices, on_device(): lax.all_to_all(jnp.where(present[..., None], picked, jnp.zeros((), table....  58.5 us
    all_to_all x1, waiting for transfers between devices, on_device(): lax.all_to_all(outgoing.reshape(owners, slot_count, width_here), ('sectio...  53.7 us
    all_to_all x1, blocking collectives, on_device(): lax.all_to_all(requests, ('section', 'wide'), split_axis=0, concat_axis=0...  35 us
    reduce_scatter x1, waiting for transfers between devices, on_device(): lax.psum_scatter(partial_value, 'narrow', scatter_dimension=1, tiled=True)  26.5 us
    all_to_all x1, starting transfers between devices, on_device(): lax.all_to_all(outgoing.reshape(owners, slot_count, width_here), ('sectio...  23.3 us
    all_gather x1, blocking collectives, on_device(): residual_full = lax.all_gather(residual, 'narrow', axis=1, tiled=True)  10.7 us
    psum x1, blocking collectives, on_device(): lax.psum(jnp.sum(rows_float * rows_float, axis=1), 'narrow') / D  8.48 us
  transfers between devices with their start and end apart: 4, of which 4 were waited for; matrix products, arithmetic and copies ran while one was open for 4% of the time, Pallas kernels for 0%

commit v1 on v0

v1 whole, which is shorter than its diff:
```python
import functools

import jax
import jax.numpy as jnp
from jax import lax
from jax.experimental import pallas as pl
from jax.experimental.pallas import tpu as pltpu
from jax.sharding import PartitionSpec as P

MESH = pl.DeviceIdType.MESH
D = 8192
EPSILON = 1e-05
NY, NZ, NC, NX = 4, 16, 2, 4
GROUP = NY * NZ * NC
SPLIT = 512
TILE = 256
IDS = 128


def kernel(
    shard_col,
    shard_row,
    row_col,
    target_ref,
    gain_ref,
    weight_hbm,
    table_hbm,
    out_ref,
    full,
    table,
    send_one,
    recv_one,
    send_two,
    recv_two,
    hidden,
    normed,
    own_part,
    part_out,
    part_in,
    resid,
    small_out,
    small_in,
    inner_out,
    inner_in,
    local_sem,
    table_sem,
    recv_a,
    recv_b,
    sent_a,
    sent_b,
    one_recv,
    one_sent,
    two_recv,
    two_sent,
    small_recv,
    small_sent,
    part_recv,
    part_sent,
    resid_recv,
    resid_sent,
    inner_recv,
    inner_sent,
):
    f32, bf16 = jnp.float32, jnp.bfloat16
    section, wide, x = lax.axis_index("section"), lax.axis_index("wide"), lax.axis_index("narrow")
    z, c = wide // 4, wide % 2
    y = section * 2 + (wide // 2) % 2
    slots = recv_two.shape[0] * recv_two.shape[1]
    tokens = target_ref.shape[0]
    depth = full.shape[1]
    width = full.shape[2]
    cols_a, cols_b = pl.ds(0, SPLIT), pl.ds(SPLIT, width - SPLIT)

    def device(yy, zz, cc, xx):
        return (yy // 2, zz * 4 + (yy % 2) * 2 + cc, xx)

    def block(yy, zz, cc):
        return (yy // 2) * (NZ * 4) + zz * 4 + (yy % 2) * 2 + cc

    def yy_of(step):
        return lax.rem(y + step + NY, NY)

    def zz_of(step):
        return lax.rem(z + step + NZ, NZ)

    def xx_of(step):
        return lax.rem(x + step + NX, NX)

    load_weight = pltpu.make_async_copy(weight_hbm, full.at[block(y, z, c)], local_sem)
    load_weight.start()
    load_table = pltpu.make_async_copy(table_hbm, table, table_sem)
    load_table.start()

    barrier = pltpu.get_barrier_semaphore()

    def greet_z(step, carry):
        pl.semaphore_signal(barrier, inc=1, device_id=device(y, zz_of(step), c, x), device_id_type=MESH)
        return carry

    lax.fori_loop(1, NZ, greet_z, 0)
    here = y * 2 + c

    def greet_y(step, carry):
        other = lax.rem(here + step, NY * NC)
        pl.semaphore_signal(barrier, inc=1, device_id=device(other // 2, z, other % 2, x), device_id_type=MESH)
        return carry

    lax.fori_loop(1, NY * NC, greet_y, 0)
    for step in range(1, NX):
        pl.semaphore_signal(barrier, inc=1, device_id=device(y, z, c, xx_of(step)), device_id_type=MESH)

    holder = shard_row[...]
    earlier = lax.broadcasted_iota(jnp.int32, (tokens, tokens), 0) < lax.broadcasted_iota(
        jnp.int32, (tokens, tokens), 1
    )
    same = jnp.logical_and(shard_col[...] == holder, earlier)
    rank = jnp.sum(jnp.where(same, 1.0, 0.0), axis=0, keepdims=True).astype(jnp.int32)
    hold_z = (holder // 4) % NZ
    hold_y = (holder // 64) * 4 + holder % 4
    slot_of = hold_z * (NY * NC * 2) + hold_y * 2 + rank
    place = jnp.where(lax.broadcasted_iota(jnp.int32, (slots, tokens), 0) == slot_of, 1.0, 0.0).astype(bf16)
    lane = lax.broadcasted_iota(jnp.int32, (tokens, IDS), 1)
    row = row_col[...]
    ids = jnp.where(lane == 0, row // 16 + 1, jnp.where(lane == 1, row % 16, 0)).astype(f32).astype(bf16)
    kept = target_ref.shape[1]
    per_z = slots // NZ
    payload = jnp.dot(place, target_ref[...], preferred_element_type=f32).astype(bf16)
    send_one[:, :, 0:kept] = payload.reshape(NZ, per_z, kept)
    payload_ids = jnp.dot(place, ids, preferred_element_type=f32).astype(bf16)
    send_one[:, :, kept:] = payload_ids.reshape(NZ, per_z, IDS)

    pl.semaphore_wait(barrier, (NZ - 1) + (NY * NC - 1) + (NX - 1))

    def copy_one(to_z, from_z):
        return pltpu.make_async_remote_copy(
            src_ref=send_one.at[to_z],
            dst_ref=recv_one.at[from_z],
            send_sem=one_sent,
            recv_sem=one_recv.at[from_z],
            device_id=device(y, to_z, c, x),
            device_id_type=MESH,
        )

    def start_one(step, carry):
        copy_one(zz_of(step), z).start()
        return carry

    lax.fori_loop(1, NZ, start_one, 0)

    def copy_weight(which, yy, zz, cc, to):
        cols, recv, sent = (cols_a, recv_a, sent_a) if which == "a" else (cols_b, recv_b, sent_b)
        piece = full.at[block(yy, zz, cc), :, cols]
        return pltpu.make_async_remote_copy(
            src_ref=piece,
            dst_ref=piece,
            send_sem=sent,
            recv_sem=recv.at[block(yy, zz, cc)],
            device_id=to,
            device_id_type=MESH,
        )

    above, below = device(yy_of(1), z, c, x), device(yy_of(-1), z, c, x)
    opposite = device(yy_of(2), z, c, x)
    after, before = device(y, zz_of(1), c, x), device(y, zz_of(-1), c, x)
    partner = device(y, z, 1 - c, x)

    def pass_on(which, yy, zz, targets):
        for to in targets:
            copy_weight(which, yy, zz, c, to).start()

    def arrive(which, yy, zz, cc):
        copy_weight(which, yy, zz, cc, partner).wait_recv()

    load_weight.wait()
    pass_on("b", y, z, (after, before, above, below, partner))
    pass_on("a", y, z, (after, before, above, below, opposite, partner))
    recv_one[z] = send_one[z]
    for step in range(1, NY):
        arrive("a", yy_of(step), z, c)
        pass_on("a", yy_of(step), z, (after, before, partner))

    def first_hand(distance, sign, ahead):
        zz = zz_of(sign * distance)
        onward = after if sign < 0 else before
        arrive("b", y, zz, c)
        if ahead is True:
            pass_on("b", y, zz, (onward,))
        elif ahead is not None:
            pl.when(ahead)(lambda: pass_on("b", y, zz, (onward,)))
        pass_on("b", y, zz, (above, below, partner))
        for step in range(NY):
            arrive("a", yy_of(step), zz, c)
            if ahead is True:
                pass_on("a", yy_of(step), zz, (onward,))
            elif ahead is not None:
                pl.when(ahead)(functools.partial(pass_on, "a", yy_of(step), zz, (onward,)))
            pass_on("a", yy_of(step), zz, (partner,))

    def second_hand(distance, sign):
        zz = zz_of(sign * distance)
        arrive("b", yy_of(-1), zz, c)
        pl.when(distance % 2 == 0)(lambda: pass_on("b", yy_of(-1), zz, (above,)))
        pass_on("b", yy_of(-1), zz, (partner,))
        arrive("b", yy_of(1), zz, c)
        pl.when(distance % 2 == 1)(lambda: pass_on("b", yy_of(1), zz, (below,)))
        pass_on("b", yy_of(1), zz, (partner,))

    def third_hand(distance, sign):
        zz = zz_of(sign * distance)
        arrive("b", yy_of(2), zz, c)
        pass_on("b", yy_of(2), zz, (partner,))

    def spread(distance, carry):
        first_hand(distance, -1, True)
        first_hand(distance, 1, distance < NZ // 2 - 1)
        second_hand(distance - 1, -1)
        pl.when(distance > 1)(lambda: second_hand(distance - 1, 1))
        pl.when(distance > 1)(lambda: third_hand(distance - 2, -1))
        pl.when(distance > 2)(lambda: third_hand(distance - 2, 1))
        return carry

    lax.fori_loop(1, 4, spread, 0)

    def wait_one(step, carry):
        copy_one(z, zz_of(step)).wait_recv()
        return carry

    lax.fori_loop(1, NZ, wait_one, 0)
    out_slot = lax.broadcasted_iota(jnp.int32, (slots, slots), 0)
    in_slot = lax.broadcasted_iota(jnp.int32, (slots, slots), 1)
    per_y = slots // (NY * NC)
    from_slot = ((out_slot % per_y) // 2) * per_z + (out_slot // per_y) * 2 + out_slot % 2
    order = jnp.where(in_slot == from_slot, 1.0, 0.0).astype(bf16)
    arrived = recv_one[...].reshape(slots, kept + IDS)
    send_two[...] = (
        jnp.dot(order, arrived, preferred_element_type=f32).astype(bf16).reshape(NY * NC, per_y, kept + IDS)
    )

    def copy_two(to_y, from_y):
        return pltpu.make_async_remote_copy(
            src_ref=send_two.at[to_y],
            dst_ref=recv_two.at[from_y],
            send_sem=two_sent,
            recv_sem=two_recv.at[from_y],
            device_id=device(to_y // 2, z, to_y % 2, x),
            device_id_type=MESH,
        )

    def start_two(step, carry):
        copy_two(lax.rem(here + step, NY * NC), here).start()
        return carry

    lax.fori_loop(1, NY * NC, start_two, 0)
    recv_two[here] = send_two[here]

    lax.fori_loop(4, 6, spread, 0)

    def wait_two(step, carry):
        copy_two(here, lax.rem(here + step, NY * NC)).wait_recv()
        return carry

    lax.fori_loop(1, NY * NC, wait_two, 0)

    load_table.wait()
    rows_here = table.shape[0]
    named = recv_two[:, :, kept:].reshape(slots, IDS).astype(f32)
    wanted = (named[:, 0:1] - 1.0) * 16.0 + named[:, 1:2]
    pick = jnp.where(
        lax.broadcasted_iota(jnp.int32, (slots, rows_here), 1).astype(f32) == wanted, 1.0, 0.0
    ).astype(bf16)
    square_sum = jnp.zeros((slots, 1), f32)
    for tile in range(width // 512):
        at = pl.ds(tile * 512, 512)
        picked = jnp.dot(pick, table[:, at], preferred_element_type=f32)
        hidden[:, at] = picked.astype(bf16)
        square_sum += jnp.sum(picked * picked, axis=1, keepdims=True)
    diagonal = out_slot == in_slot

    def as_row(column):
        return jnp.sum(jnp.where(diagonal, column, 0.0), axis=0, keepdims=True)

    def as_column(line):
        return jnp.sum(jnp.where(diagonal, line, 0.0), axis=1, keepdims=True)

    def copy_small(source, landing, sent, recv, step):
        return pltpu.make_async_remote_copy(
            src_ref=source,
            dst_ref=landing.at[step - 1],
            send_sem=sent.at[step - 1],
            recv_sem=recv.at[step - 1],
            device_id=device(y, z, c, xx_of(step)),
            device_id_type=MESH,
        )

    square_row = as_row(square_sum)
    small_out[...] = jnp.broadcast_to(square_row, small_out.shape)
    for step in range(1, NX):
        copy_small(small_out, small_in, small_sent, small_recv, step).start()

    lax.fori_loop(6, 8, spread, 0)
    half = NZ // 2
    first_hand(half, -1, None)
    for sign in (-1, 1):
        second_hand(half - 1, sign)
        third_hand(half - 2, sign)

    for step in range(1, NX):
        copy_small(small_out, small_in, small_sent, small_recv, step).wait_recv()
    total = square_row
    for step in range(1, NX):
        total += small_in[step - 1][0:1, :]
    row_scale = lax.rsqrt(as_column(total) / D + EPSILON)
    for tile in range(width // 512):
        at = pl.ds(tile * 512, 512)
        normed[:, at] = (hidden[:, at].astype(f32) * row_scale * gain_ref[:, at]).astype(bf16)

    second_hand(half, -1)
    for sign in (-1, 1):
        third_hand(half - 1, sign)
    third_hand(half, -1)

    def wait_partner(zz, carry):
        for yy in range(NY):
            arrive("a", yy, zz, 1 - c)
            arrive("b", yy, zz, 1 - c)
        return carry

    lax.fori_loop(0, NZ, wait_partner, 0)

    blocks = TILE // depth
    tiles_x = kept // TILE

    def project(tile):
        rows = full[pl.ds(tile * blocks, blocks)].reshape(TILE, width)
        return lax.dot_general(normed[...], rows, (((1,), (1,)), ((), ())), preferred_element_type=f32)

    def copy_part(step, part):
        return pltpu.make_async_remote_copy(
            src_ref=part_out.at[step - 1, part],
            dst_ref=part_in.at[step - 1, part],
            send_sem=part_sent.at[step - 1, part],
            recv_sem=part_recv.at[step - 1, part],
            device_id=device(y, z, c, xx_of(step)),
            device_id_type=MESH,
        )

    for step in (2, 1, 3):
        for part in range(tiles_x):
            part_out[step - 1, part] = project(xx_of(step) * tiles_x + part).astype(bf16)
            copy_part(step, part).start()
    for part in range(tiles_x):
        own_part[part] = project(x * tiles_x + part)

    def copy_resid(step, part):
        return pltpu.make_async_remote_copy(
            src_ref=resid.at[x, part],
            dst_ref=resid.at[x, part],
            send_sem=resid_sent.at[step - 1, part],
            recv_sem=resid_recv.at[step - 1, part],
            device_id=device(y, z, c, xx_of(step)),
            device_id_type=MESH,
        )

    inner = jnp.zeros((slots, 1), f32)
    for part in range(tiles_x):
        projected = own_part[part]
        for step in range(1, NX):
            copy_part(step, part).wait_recv()
            projected += part_in[step - 1, part].astype(f32)
        goal = recv_two[:, :, part * TILE : (part + 1) * TILE].reshape(slots, TILE)
        residual = (projected - goal.astype(f32)).astype(bf16)
        resid[x, part] = residual
        for step in (2, 1, 3):
            copy_resid(step, part).start()
        inner += jnp.sum(projected * residual.astype(f32), axis=1, keepdims=True)
    inner_row = as_row(inner)
    inner_out[...] = jnp.broadcast_to(inner_row, inner_out.shape)
    for step in range(1, NX):
        copy_small(inner_out, inner_in, inner_sent, inner_recv, step).start()

    def landed(step, part):
        return pltpu.make_async_remote_copy(
            src_ref=resid.at[xx_of(-step), part],
            dst_ref=resid.at[xx_of(-step), part],
            send_sem=resid_sent.at[step - 1, part],
            recv_sem=resid_recv.at[step - 1, part],
            device_id=device(y, z, c, xx_of(step)),
            device_id_type=MESH,
        )

    for step in range(1, NX):
        for part in range(tiles_x):
            landed(step, part).wait_recv()
    for step in range(1, NX):
        copy_small(inner_out, inner_in, inner_sent, inner_recv, step).wait_recv()
    inner_all = inner_row
    for step in range(1, NX):
        inner_all += inner_in[step - 1][0:1, :]
    pull = row_scale * row_scale * as_column(inner_all) / D
    wanted_row = as_row(wanted)
    put = jnp.where(
        lax.broadcasted_iota(jnp.int32, (rows_here, slots), 0).astype(f32) == wanted_row, 1.0, 0.0
    ).astype(bf16)

    def finish(tile, carry):
        at = pl.ds(pl.multiple_of(tile * TILE, TILE), TILE)
        back = jnp.zeros((slots, TILE), f32)
        for index in range(NX * tiles_x):
            rows = full[pl.ds(index * blocks, blocks), :, at].reshape(TILE, TILE)
            back += jnp.dot(resid[index // tiles_x, index % tiles_x], rows, preferred_element_type=f32)
        weighted = back * gain_ref[:, at]
        grad = (row_scale * weighted - hidden[:, at].astype(f32) * pull).astype(bf16)
        out_ref[:, at] = jnp.dot(put, grad, preferred_element_type=f32).astype(bf16)
        return carry

    lax.fori_loop(0, width // TILE, finish, 0)

    def all_sent(ref, sem):
        pltpu.make_async_copy(ref, ref, sem).wait()

    all_sent(full.at[pl.ds(0, GROUP - 1), :, cols_a], sent_a)
    all_sent(full.at[pl.ds(0, GROUP - 1), :, cols_b], sent_b)
    all_sent(send_one.at[pl.ds(0, NZ - 1)], one_sent)
    all_sent(send_two.at[pl.ds(0, NY * NC - 1)], two_sent)
    for step in range(1, NX):
        copy_small(small_out, small_in, small_sent, small_recv, step).wait_send()
        copy_small(inner_out, inner_in, inner_sent, inner_recv, step).wait_send()
        for part in range(tiles_x):
            copy_part(step, part).wait_send()
            copy_resid(step, part).wait_send()


def on_device(token_shard, token_row, table, gain, key_value_weight, kv_target):
    tokens = token_row.shape[0]
    depth, width = key_value_weight.shape
    kept = kv_target.shape[1]
    slots = 2 * tokens
    parts = kept // TILE
    bf16, f32 = jnp.bfloat16, jnp.float32
    dma = pltpu.SemaphoreType.DMA
    vmem = pl.BlockSpec(memory_space=pltpu.VMEM)
    anywhere = pl.BlockSpec(memory_space=pl.ANY)
    return pl.pallas_call(
        kernel,
        out_shape=jax.ShapeDtypeStruct(table.shape, bf16),
        in_specs=[vmem] * 5 + [anywhere] * 2,
        out_specs=vmem,
        scratch_shapes=[
            pltpu.VMEM((GROUP, depth, width), bf16),
            pltpu.VMEM(table.shape, bf16),
            pltpu.VMEM((NZ, slots // NZ, kept + IDS), bf16),
            pltpu.VMEM((NZ, slots // NZ, kept + IDS), bf16),
            pltpu.VMEM((NY * NC, slots // (NY * NC), kept + IDS), bf16),
            pltpu.VMEM((NY * NC, slots // (NY * NC), kept + IDS), bf16),
            pltpu.VMEM((slots, width), bf16),
            pltpu.VMEM((slots, width), bf16),
            pltpu.VMEM((parts, slots, TILE), f32),
            pltpu.VMEM((NX - 1, parts, slots, TILE), bf16),
            pltpu.VMEM((NX - 1, parts, slots, TILE), bf16),
            pltpu.VMEM((NX, parts, slots, TILE), bf16),
            pltpu.VMEM((8, slots), f32),
            pltpu.VMEM((NX - 1, 8, slots), f32),
            pltpu.VMEM((8, slots), f32),
            pltpu.VMEM((NX - 1, 8, slots), f32),
            dma,
            dma,
            dma((GROUP,)),
            dma((GROUP,)),
            dma,
            dma,
            dma((NZ,)),
            dma,
            dma((NY * NC,)),
            dma,
            dma((NX - 1,)),
            dma((NX - 1,)),
            dma((NX - 1, parts)),
            dma((NX - 1, parts)),
            dma((NX - 1, parts)),
            dma((NX - 1, parts)),
            dma((NX - 1,)),
            dma((NX - 1,)),
        ],
        compiler_params=pltpu.CompilerParams(
            collective_id=0, has_side_effects=True, vmem_limit_bytes=48 * 2**20
        ),
    )(
        token_shard,
        token_shard.reshape(1, tokens),
        token_row.reshape(tokens, 1),
        kv_target,
        gain.reshape(1, width),
        key_value_weight,
        table,
    )


def solution(mesh):
    return jax.shard_map(
        on_device,
        mesh=mesh,
        in_specs=(
            P(("section", "wide"), None),
            P(("section", "wide")),
            P(("section", "wide"), "narrow"),
            P("narrow"),
            P(("section", "wide"), "narrow"),
            P(("section", "wide"), "narrow"),
        ),
        out_specs=P(("section", "wide"), "narrow"),
        check_vma=False,
    )
```

time: 418 us -> 114 us (0.27)
  waiting for transfers between devices: 269 us -> 0 us
  Pallas kernels: 0 us -> 106 us
  blocking collectives: 60.2 us -> 0 us
  starting transfers between devices: 31.1 us -> 0 us
  matrix products: 16.4 us -> 0 us
  between operations: 13.6 us -> 0.02 us
  other arithmetic: 12.9 us -> 0 us
  local copies, waits for them, and re-layouts: 14.8 us -> 7.52 us
    all_gather x1 -> x0, waiting for transfers between devices: 129 us -> none  [on_device(): lax.all_gather(key_value_weight, ('section', 'wide'), axis=0, tiled=True)]
    all_to_all x2 -> x0, waiting for transfers between devices: 112 us -> none  [the longest x1 58.5 us: on_device(): lax.all_to_all(jnp.where(present[..., None], picked, jnp.zeros((), table....]
    pallas_call x0 -> x1, Pallas kernels: none -> 106 us  [on_device(): pl.pallas_call(kernel, out_shape=jax.ShapeDtypeStruct(table.shape, bf16),...]
    all_to_all x1 -> x0, blocking collectives: 35 us -> none  [on_device(): lax.all_to_all(requests, ('section', 'wide'), split_axis=0, concat_axis=0...]
    all_to_all x2 -> x0, starting transfers between devices: 31.1 us -> none  [the longest x1 23.3 us: on_device(): lax.all_to_all(outgoing.reshape(owners, slot_count, width_here), ('sectio...]
    reduce_scatter x1 -> x0, waiting for transfers between devices: 26.5 us -> none  [on_device(): lax.psum_scatter(partial_value, 'narrow', scatter_dimension=1, tiled=True)]
    dot_general x3 -> x0, matrix products: 16.4 us -> none  [the longest x1 7.44 us: contract_last(): lax.dot_general(left, right, (((1,), (1,)), ((), ())), preferred_element_...]
    psum x2 -> x0, blocking collectives: 14.5 us -> none  [the longest x1 8.48 us: on_device(): lax.psum(jnp.sum(rows_float * rows_float, axis=1), 'narrow') / D]
  transfers between devices with their start and end apart: 4 -> 0, of which waited for: 4 -> 0; matrix products, arithmetic and copies ran while one was open for 4% -> 0% of each run, Pallas kernels for 0% -> 0%
where the time goes in v1:
time: 114 us
  Pallas kernels  106 us (93%)
  local copies, waits for them, and re-layouts  7.52 us (7%)
    pallas_call x1, Pallas kernels, on_device(): pl.pallas_call(kernel, out_shape=jax.ShapeDtypeStruct(table.shape, bf16),...  106 us
    unnamed x12, local copies, waits for them, and re-layouts  6.76 us

profile of v1, /device:TPU:1, one launch (start us, length us, event | category | flops | bytes accessed | tf_op | source)
XLA Modules:
  0.0 113.8 jit_solution(16413322061981818183)
XLA Ops:
  0.0 0.8 copy.8.row_col
  0.8 0.8 copy.7.shard_col
  1.5 0.0 copy-start
  1.5 1.6 %copy-done = bf16[512,2048]{1,0:T(8,128)(2,1)S(1)} copy-done((bf16[512,2048]{1,0:T(8,128)(2,1)S(1)}, bf16[512,2048]{1,0:T(8,128)(2,1)}, u32[]{:S(2)}) %copy-start) | copy-done | bytes 2097176
  3.1 0.0 copy-start.1
  3.1 0.9 copy-done.1
  4.0 0.0 copy-start.2
  4.0 0.8 copy-done.2
  4.9 0.0 copy-start.3
  4.9 0.7 copy-done.3
  5.6 0.0 copy-start.4
  5.6 0.7 copy-done.4
  6.2 106.3 %shard_map.64 = bf16[512,2048]{1,0:T(8,128)(2,1)S(1)} custom-call(s32[128,1]{1,0:T(8,128)S(1)} %copy.7.shard_col, s32[1,128]{1,0:T(1,128)S(1)} %bitcast.4, s32[128,1]{1,0:T(8,128)S(1)} %copy.8.row_col, bf16[128,512]{1,0:T(8,128)(2,1)S(1)} %copy-done.1, f32[1,2048]{1,0:T(1,128)S(1)} %bitcast.3, bf16[16,2048]{1,0:T(8,128)(2,1)S(1)} %copy-done.2, ...), custom_call_target="tpu_custom_call" | custom-call | tf_op jit(solution)/shard_map/pallas_call | solution.py:443
  112.5 1.3 %copy.10 = bf16[512,2048]{1,0:T(8,128)(2,1)} copy(bf16[512,2048]{1,0:T(8,128)(2,1)S(1)} %shard_map.64) | data formatting | bytes 4194304
Async XLA Ops:
  1.5 1.6 %copy-start = (bf16[512,2048]{1,0:T(8,128)(2,1)S(1)}, bf16[512,2048]{1,0:T(8,128)(2,1)}, u32[]{:S(2)}) copy-start(bf16[512,2048]{1,0:T(8,128)(2,1)} %table_hbm.1) | copy-start | bytes 6291460
  3.1 0.9 copy-start.1
  4.0 0.8 copy-start.2
  4.9 0.7 copy-start.3
  5.6 0.7 copy-start.4

commit v2 on v0

v2 whole, which is shorter than its diff:
```python
import functools

import jax
import jax.numpy as jnp
from jax import lax
from jax.experimental import pallas as pl
from jax.experimental.pallas import tpu as pltpu
from jax.sharding import PartitionSpec as P

MESH = pl.DeviceIdType.MESH
D = 8192
EPSILON = 1e-05
NY, NZ, NC, NX = 4, 16, 2, 4
GROUP = NY * NZ * NC
SPLIT = 512
TILE = 256
PART = 128
HALF = 128
TURNS = 8


def kernel(
    shard_hbm,
    row_hbm,
    target_hbm,
    gain_hbm,
    weight_hbm,
    table_hbm,
    out_ref,
    shard,
    row,
    target,
    gain,
    full,
    table,
    ids_out,
    ids_mid,
    ids_all,
    ids_in,
    goal_out,
    goal_mid,
    goal_next,
    goal,
    hidden,
    normed,
    partial,
    half_out,
    half_in,
    joint_out,
    joint_in,
    resid,
    inner,
    back,
    square_out,
    square_in,
    inner_out,
    inner_in,
    local_sem,
    recv_a,
    recv_b,
    sent_a,
    sent_b,
    idy_recv,
    idz_recv,
    goaly_recv,
    goalz_recv,
    many_sent,
    square_recv,
    square_sent,
    inner_recv,
    inner_sent,
    half_recv,
    half_sent,
    joint_recv,
    joint_sent,
    resid_recv,
    resid_sent,
):
    f32, bf16, i32 = jnp.float32, jnp.bfloat16, jnp.int32
    section, wide, x = lax.axis_index("section"), lax.axis_index("wide"), lax.axis_index("narrow")
    z, c = wide // 4, wide % 2
    y = section * 2 + (wide // 2) % 2
    here = y * 2 + c
    tokens, kept = target.shape
    slots = normed.shape[0]
    depth, width = full.shape[1:]
    rows_here = table.shape[0]
    cols_a, cols_b = pl.ds(0, SPLIT), pl.ds(SPLIT, width - SPLIT)
    spots = NY * NC
    per_y, per_z = slots // spots, slots // NZ

    def device(yy, zz, cc, xx):
        return (yy // 2, zz * 4 + (yy % 2) * 2 + cc, xx)

    def block(yy, zz, cc):
        return (yy // 2) * (NZ * 4) + zz * 4 + (yy % 2) * 2 + cc

    def yy_of(step):
        return lax.rem(y + step + NY, NY)

    def zz_of(step):
        return lax.rem(z + step + NZ, NZ)

    def xx_of(step):
        return lax.rem(x + step + NX, NX)

    def beside(xx):
        return device(y, z, c, xx)

    def remote(source, landing, sent, recv, to):
        return pltpu.make_async_remote_copy(
            src_ref=source, dst_ref=landing, send_sem=sent, recv_sem=recv, device_id=to, device_id_type=MESH
        )

    loads = [
        pltpu.make_async_copy(source, landing, local_sem.at[number])
        for number, (source, landing) in enumerate(
            (
                (shard_hbm, shard),
                (row_hbm, row),
                (weight_hbm, full.at[block(y, z, c)]),
                (target_hbm, target),
                (gain_hbm, gain),
                (table_hbm, table),
            )
        )
    ]
    for load in loads:
        load.start()

    barrier = pltpu.get_barrier_semaphore()

    def greet_z(step, carry):
        pl.semaphore_signal(barrier, inc=1, device_id=device(y, zz_of(step), c, x), device_id_type=MESH)
        return carry

    lax.fori_loop(1, NZ, greet_z, 0)

    def greet_y(step, carry):
        other = lax.rem(here + step, spots)
        pl.semaphore_signal(barrier, inc=1, device_id=device(other // 2, z, other % 2, x), device_id_type=MESH)
        return carry

    lax.fori_loop(1, spots, greet_y, 0)
    for step in range(1, NX):
        pl.semaphore_signal(barrier, inc=1, device_id=beside(xx_of(step)), device_id_type=MESH)

    loads[0].wait()
    loads[1].wait()
    first = lax.broadcasted_iota(i32, (tokens, tokens), 0)
    second = lax.broadcasted_iota(i32, (tokens, tokens), 1)
    holder = shard[...]
    holder_col = jnp.sum(jnp.where(first == second, holder, 0), axis=1, keepdims=True)
    same = jnp.logical_and(holder_col == holder, first < second)
    rank = jnp.sum(jnp.where(same, 1, 0), axis=0, keepdims=True)
    hold_z = (holder // 4) % NZ
    hold_y = (holder // 64) * 4 + holder % 4
    slot_of = hold_y * per_y + hold_z * 2 + rank
    placed = lax.broadcasted_iota(i32, (slots, tokens), 0) == slot_of
    slot_id = jnp.sum(jnp.where(placed, row[...] + 1, 0), axis=1, keepdims=True).astype(f32)
    spread_ids = lax.broadcasted_iota(i32, (per_y, 128), 0) == lax.broadcasted_iota(i32, (per_y, 128), 1)
    for spot in range(spots):
        line = jnp.sum(
            jnp.where(spread_ids, slot_id[spot * per_y : (spot + 1) * per_y], 0.0), axis=0, keepdims=True
        )
        ids_out[spot] = jnp.broadcast_to(line, (8, 128))
    loads[3].wait()
    place = jnp.where(placed, 1.0, 0.0).astype(bf16)
    goal_out[...] = (
        jnp.dot(place, target[...], preferred_element_type=f32).astype(bf16).reshape(spots, per_y, kept)
    )
    loads[2].wait()

    pl.semaphore_wait(barrier, (NZ - 1) + (spots - 1) + (NX - 1))

    def spot_device(spot):
        return device(spot // 2, z, spot % 2, x)

    def copy_idy(to, source):
        return remote(ids_out.at[to], ids_mid.at[source], many_sent.at[0], idy_recv.at[source], spot_device(to))

    def copy_idz(to, source):
        return remote(ids_all, ids_in.at[source], many_sent.at[1], idz_recv.at[source], device(y, to, c, x))

    def copy_goaly(to, source):
        return remote(goal_out.at[to], goal_mid.at[source], many_sent.at[2], goaly_recv.at[source], spot_device(to))

    def copy_goalz(to, source):
        return remote(goal_next.at[to], goal.at[source], many_sent.at[3], goalz_recv.at[source], device(y, to, c, x))

    def copy_weight(which, yy, zz, cc, to):
        cols, recv, sent = (cols_a, recv_a, sent_a) if which == "a" else (cols_b, recv_b, sent_b)
        piece = full.at[block(yy, zz, cc), :, cols]
        return remote(piece, piece, sent, recv.at[block(yy, zz, cc)], to)

    above, below = device(yy_of(1), z, c, x), device(yy_of(-1), z, c, x)
    opposite = device(yy_of(2), z, c, x)
    after, before = device(y, zz_of(1), c, x), device(y, zz_of(-1), c, x)
    partner = device(y, z, 1 - c, x)

    def pass_on(which, yy, zz, targets):
        for to in targets:
            copy_weight(which, yy, zz, c, to).start()

    def arrive(which, yy, zz, cc):
        copy_weight(which, yy, zz, cc, partner).wait_recv()

    def each(low, high, act):
        def step(index, carry):
            act(index)
            return carry

        lax.fori_loop(low, high, step, 0)

    def around(step):
        return lax.rem(here + step, spots)

    pass_on("b", y, z, (after, before))
    pass_on("a", y, z, (above, below, opposite))
    each(1, spots, lambda step: copy_idy(around(step), here).start())
    each(1, spots, lambda step: copy_goaly(around(step), here).start())
    pass_on("b", y, z, (above, below))
    pass_on("a", y, z, (after, before, partner))
    pass_on("b", y, z, (partner,))
    ids_mid[here] = ids_out[here]
    goal_mid[here] = goal_out[here]

    def when(condition, act):
        if isinstance(condition, bool):
            if condition:
                act()
        else:
            pl.when(condition)(act)

    def onward(which, yy, zz, sign, ahead):
        to = after if sign < 0 else before
        when(ahead, lambda: pass_on(which, yy, zz, (to,)))

    def first_hand(distance, sign, ahead):
        zz = zz_of(sign * distance)
        arrive("b", y, zz, c)
        onward("b", y, zz, sign, ahead)
        pass_on("b", y, zz, (above, below, partner))

    def planes(distance, sign, ahead):
        zz = zz_of(sign * distance)
        for step in range(NY):
            arrive("a", yy_of(step), zz, c)
            onward("a", yy_of(step), zz, sign, ahead)
            pass_on("a", yy_of(step), zz, (partner,))

    def second_hand(distance, sign):
        zz = zz_of(sign * distance)
        arrive("b", yy_of(-1), zz, c)
        when(distance % 2 == 0, lambda: pass_on("b", yy_of(-1), zz, (above,)))
        pass_on("b", yy_of(-1), zz, (partner,))
        arrive("b", yy_of(1), zz, c)
        when(distance % 2 == 1, lambda: pass_on("b", yy_of(1), zz, (below,)))
        pass_on("b", yy_of(1), zz, (partner,))

    def third_hand(distance, sign):
        zz = zz_of(sign * distance)
        arrive("b", yy_of(2), zz, c)
        pass_on("b", yy_of(2), zz, (partner,))

    def later(hand, distance):
        if isinstance(distance, int):
            if distance >= 0:
                hand(distance, -1)
            if 1 <= distance < NZ // 2:
                hand(distance, 1)
            return
        pl.when(distance >= 0)(lambda: hand(distance, -1))
        pl.when(distance >= 1)(lambda: hand(distance, 1))

    def send_goal(step):
        copy_goalz(zz_of(step), z).start()

    def spread(distance):
        first_hand(distance, -1, True)
        first_hand(distance, 1, distance < NZ // 2 - 1)

        @pl.when(distance <= 4)
        def _():
            for step in (11, 10):
                send_goal(step - 2 * distance)
                send_goal(2 * distance - step)

        planes(distance - 1, -1, True)
        planes(distance - 1, 1, True)
        later(second_hand, distance - 1)
        later(third_hand, distance - 2)

    first_hand(1, -1, True)
    first_hand(1, 1, True)
    each(1, spots, lambda step: copy_idy(here, around(step)).wait_recv())
    ids_all[...] = jnp.concatenate([ids_mid[spot][0:1, :] for spot in range(spots)], axis=0)
    each(1, NZ, lambda step: copy_idz(zz_of(step), z).start())
    ids_in[z] = ids_all[...]
    for step in range(1, NY):
        arrive("a", yy_of(step), z, c)
        pass_on("a", yy_of(step), z, (after, before, partner))

    each(1, spots, lambda step: copy_goaly(here, around(step)).wait_recv())
    out_slot = lax.broadcasted_iota(i32, (slots, slots), 0)
    in_slot = lax.broadcasted_iota(i32, (slots, slots), 1)
    inside = out_slot % per_z
    from_slot = (inside % spots) * per_y + (out_slot // per_z) * 2 + inside // spots
    order = jnp.where(in_slot == from_slot, 1.0, 0.0).astype(bf16)
    arrived = goal_mid[...].reshape(slots, kept)
    goal_next[...] = jnp.dot(order, arrived, preferred_element_type=f32).astype(bf16).reshape(NZ, per_z, kept)
    send_goal(NZ // 2)
    goal[z] = goal_next[z]

    second_hand(0, -1)
    each(2, 3, spread)

    each(1, NZ, lambda step: copy_idz(z, zz_of(step)).wait_recv())
    loads[5].wait()
    loads[4].wait()
    listed = ids_in[...].reshape(NZ * spots, 128)
    lane = lax.broadcasted_iota(i32, listed.shape, 1)
    wanted = (
        jnp.concatenate(
            [
                jnp.sum(jnp.where(lane == 2 * z + k, listed, 0.0), axis=1, keepdims=True).reshape(NZ, spots, 1)
                for k in range(2)
            ],
            axis=1,
        ).reshape(slots, 1)
        - 1.0
    )
    pick = jnp.where(lax.broadcasted_iota(i32, (slots, rows_here), 1).astype(f32) == wanted, 1.0, 0.0).astype(bf16)
    square_sum = jnp.zeros((slots, 1), f32)
    for tile in range(width // 512):
        at = pl.ds(tile * 512, 512)
        picked = jnp.dot(pick, table[:, at], preferred_element_type=f32)
        hidden[:, at] = picked.astype(bf16)
        square_sum += jnp.sum(picked * picked, axis=1, keepdims=True)
    diagonal = out_slot == in_slot

    def as_row(column):
        return jnp.sum(jnp.where(diagonal, column, 0.0), axis=0, keepdims=True)

    def as_column(line):
        return jnp.sum(jnp.where(diagonal, line, 0.0), axis=1, keepdims=True)

    def copy_square(step):
        return remote(
            square_out, square_in.at[step - 1], square_sent.at[step - 1], square_recv.at[step - 1], beside(xx_of(step))
        )

    def copy_inner(step):
        return remote(
            inner_out, inner_in.at[step - 1], inner_sent.at[step - 1], inner_recv.at[step - 1], beside(xx_of(step))
        )

    square_row = as_row(square_sum)
    square_out[...] = jnp.broadcast_to(square_row, square_out.shape)
    for step in range(1, NX):
        copy_square(step).start()

    each(3, 4, spread)

    for step in range(1, NX):
        copy_square(step).wait_recv()
    total = square_row
    for step in range(1, NX):
        total += square_in[step - 1][0:1, :]
    row_scale = lax.rsqrt(as_column(total) / D + EPSILON)
    for tile in range(width // 512):
        at = pl.ds(tile * 512, 512)
        normed[:, at] = (hidden[:, at].astype(f32) * row_scale * gain[:, at]).astype(bf16)

    pairs = NZ // 2
    mine, lean = z // 2, 1 - 2 * (z % 2)
    pair_at = [
        lax.rem(mine + lean * (-((turn + 1) // 2) if turn % 2 else turn // 2) + pairs, pairs) for turn in range(TURNS)
    ]
    blocks = PART // depth
    right, left = xx_of(1), xx_of(-1)

    def tile_rows(part, pair):
        return pl.ds((part * pairs + pair) * blocks, blocks)

    def ends_here(pair):
        return x % 2 == pair // (pairs // 2)

    def copy_half(turn, side):
        return remote(
            half_out.at[turn, side],
            half_in.at[turn, side],
            half_sent.at[turn, side],
            half_recv.at[turn, side],
            beside(left if side else right),
        )

    def copy_joint(turn, side):
        return remote(
            joint_out.at[turn, side],
            joint_in.at[turn, side],
            joint_sent.at[turn, side],
            joint_recv.at[turn, side],
            beside(left if side else right),
        )

    def part_cols(part):
        return pl.ds(pl.multiple_of(part * PART, PART), PART)

    def side_rows(side):
        return pl.ds(side * HALF, HALF)

    def copy_resid(turn, part, side):
        piece = resid.at[turn, :, part_cols(part)]
        return remote(
            piece, piece, resid_sent.at[turn, side], resid_recv.at[turn, part, 0], beside(left if side else right)
        )

    def copy_resid_half(turn, part, side):
        piece = resid.at[turn, side_rows(side), part_cols(part)]
        return remote(
            piece, piece, resid_sent.at[turn, side], resid_recv.at[turn, part, side], beside(left if side else right)
        )

    def project(turn):
        pair = pair_at[turn]
        for step in range(2):
            for yy in range(NY):
                arrive("a", yy, pair * 2 + step, 1 - c)
                arrive("b", yy, pair * 2 + step, 1 - c)
        dest = ends_here(pair)
        order = (jnp.where(dest, 1 - x // 2, right // 2), jnp.where(dest, x // 2, left // 2))
        rows = jnp.concatenate([full[tile_rows(part, pair)].reshape(PART, width) for part in order], axis=0)
        partial[turn] = lax.dot_general(normed[...], rows, (((1,), (1,)), ((), ())), preferred_element_type=f32)

        @pl.when(dest)
        def _():
            for side in range(2):
                half_out[turn, side] = partial[turn, side_rows(side), 0:PART].astype(bf16)
                copy_half(turn, side).start()

    def relay_sums(turn):
        @pl.when(jnp.logical_not(ends_here(pair_at[turn])))
        def _():
            for side in range(2):
                copy_half(turn, side).wait_recv()
                near, far, at = side_rows(side), side_rows(1 - side), slice(side * PART, (side + 1) * PART)
                joint_out[turn, side, near] = (partial[turn, near, at] + half_in[turn, side].astype(f32)).astype(bf16)
                joint_out[turn, side, far] = partial[turn, far, at].astype(bf16)
                copy_joint(turn, side).start()

    def subtract(turn):
        pair = pair_at[turn]

        @pl.when(ends_here(pair))
        def _():
            for side in range(2):
                copy_joint(turn, side).wait_recv()
            projected = partial[turn, :, PART:] + joint_in[turn, 0].astype(f32) + joint_in[turn, 1].astype(f32)
            wished = goal[:, :, part_cols(pair % (pairs // 2))].reshape(slots, PART)
            residual = (projected - wished.astype(f32)).astype(bf16)
            resid[turn, :, part_cols(x // 2)] = residual
            for side in range(2):
                copy_resid(turn, x // 2, side).start()
            inner[...] += projected * residual.astype(f32)

    def relay_resid(turn):
        @pl.when(jnp.logical_not(ends_here(pair_at[turn])))
        def _():
            copy_resid(turn, left // 2, 0).wait_recv()
            copy_resid_half(turn, left // 2, 0).start()
            copy_resid(turn, right // 2, 1).wait_recv()
            copy_resid_half(turn, right // 2, 1).start()

    def await_resid(turn):
        @pl.when(ends_here(pair_at[turn]))
        def _():
            for side in range(2):
                copy_resid_half(turn, 1 - x // 2, side).wait_recv()

    def step_back(turn, at):
        rows = jnp.concatenate(
            [full[tile_rows(part, pair_at[turn]), :, at].reshape(PART, at.size) for part in range(2)], axis=0
        )
        return jnp.dot(resid[turn], rows, preferred_element_type=f32)

    def accumulate(turns):
        for turn in turns:
            await_resid(turn)

        def add(tile):
            at = pl.ds(pl.multiple_of(tile * TILE, TILE), TILE)
            total = step_back(turns[0], at) if turns[0] == 0 else back[:, at] + step_back(turns[0], at)
            for turn in turns[1:]:
                total += step_back(turn, at)
            back[:, at] = total

        each(0, width // TILE, add)

    inner[...] = jnp.zeros(inner.shape, f32)
    far = NZ // 2
    jobs = {
        4: ((project, 0), None, None, None),
        5: ((project, 1), (relay_sums, 0), None, None),
        6: ((project, 2), (relay_sums, 1), None, (subtract, 0)),
        7: ((project, 3), (relay_sums, 2), (subtract, 1), (relay_resid, 0)),
        8: ((project, 4), (relay_sums, 3), (subtract, 2), (relay_resid, 1)),
        9: ((project, 5), (relay_sums, 4), (subtract, 3), (relay_resid, 2)),
        10: ((project, 6), (relay_sums, 5), (subtract, 4), (relay_resid, 3)),
    }

    def work(job):
        if job is not None:
            job[0](job[1])

    for distance in range(4, far + 3):
        if distance <= far:
            first_hand(distance, -1, distance < far)
            if distance < far:
                first_hand(distance, 1, distance < far - 1)
        if distance == 4:
            for step in (3, -3, 2, -2):
                send_goal(step)
        if distance == 5:
            for step in (1, -1):
                send_goal(step)
        work(jobs[distance][0])
        if distance - 1 <= far:
            planes(distance - 1, -1, distance - 1 < far)
            if distance - 1 < far:
                planes(distance - 1, 1, distance - 1 < far - 1)
        work(jobs[distance][1])
        if distance - 1 <= far:
            later(second_hand, distance - 1)
        work(jobs[distance][2])
        later(third_hand, distance - 2)
        if distance == 6:
            each(1, NZ, lambda step: copy_goalz(z, zz_of(step)).wait_recv())
        work(jobs[distance][3])
    project(7)
    relay_sums(6)
    subtract(5)
    relay_resid(4)
    accumulate((0, 1))
    relay_sums(7)
    subtract(6)
    relay_resid(5)
    subtract(7)

    inner_row = as_row(jnp.sum(inner[...], axis=1, keepdims=True))
    inner_out[...] = jnp.broadcast_to(inner_row, inner_out.shape)
    for step in range(1, NX):
        copy_inner(step).start()
    relay_resid(6)
    accumulate((2, 3, 4, 5))
    relay_resid(7)
    wanted_row = as_row(wanted)
    put = jnp.where(lax.broadcasted_iota(i32, (rows_here, slots), 0).astype(f32) == wanted_row, 1.0, 0.0).astype(bf16)
    for step in range(1, NX):
        copy_inner(step).wait_recv()
    inner_all = inner_row
    for step in range(1, NX):
        inner_all += inner_in[step - 1][0:1, :]
    pull = row_scale * row_scale * as_column(inner_all) / D
    await_resid(6)
    await_resid(7)

    def finish(tile):
        at = pl.ds(pl.multiple_of(tile * TILE, TILE), TILE)
        weighted = (back[:, at] + step_back(6, at) + step_back(7, at)) * gain[:, at]
        grad = (row_scale * weighted - hidden[:, at].astype(f32) * pull).astype(bf16)
        out_ref[:, at] = jnp.dot(put, grad, preferred_element_type=f32).astype(bf16)

    each(0, width // TILE, finish)

    def all_sent(ref, sem):
        pltpu.make_async_copy(ref, ref, sem).wait()

    all_sent(full.at[pl.ds(0, GROUP - 1), :, cols_a], sent_a)
    all_sent(full.at[pl.ds(0, GROUP - 1), :, cols_b], sent_b)
    all_sent(ids_out.at[pl.ds(0, spots - 1)], many_sent.at[0])
    all_sent(ids_in.at[pl.ds(0, NZ - 1)], many_sent.at[1])
    all_sent(goal_out.at[pl.ds(0, spots - 1)], many_sent.at[2])
    all_sent(goal_next.at[pl.ds(0, NZ - 1)], many_sent.at[3])
    for step in range(1, NX):
        copy_square(step).wait_send()
        copy_inner(step).wait_send()
    for turn in range(TURNS):
        dest = ends_here(pair_at[turn])

        @pl.when(dest)
        def _():
            for side in range(2):
                copy_half(turn, side).wait_send()
                copy_resid(turn, x // 2, side).wait_send()

        @pl.when(jnp.logical_not(dest))
        def _():
            copy_resid_half(turn, left // 2, 0).wait_send()
            copy_resid_half(turn, right // 2, 1).wait_send()
            for side in range(2):
                copy_joint(turn, side).wait_send()


def on_device(token_shard, token_row, table, gain, key_value_weight, kv_target):
    tokens = token_row.shape[0]
    depth, width = key_value_weight.shape
    kept = kv_target.shape[1]
    slots = 2 * tokens
    spots = NY * NC
    bf16, f32, i32 = jnp.bfloat16, jnp.float32, jnp.int32
    dma, vmem = pltpu.SemaphoreType.DMA, pltpu.VMEM
    outside = pl.BlockSpec(memory_space=pltpu.HBM)
    return pl.pallas_call(
        kernel,
        out_shape=jax.ShapeDtypeStruct(table.shape, bf16),
        in_specs=[outside] * 6,
        out_specs=pl.BlockSpec(memory_space=vmem),
        scratch_shapes=[
            vmem((1, tokens), i32),
            vmem((1, tokens), i32),
            vmem((tokens, kept), bf16),
            vmem((1, width), f32),
            vmem((GROUP, depth, width), bf16),
            vmem(table.shape, bf16),
            vmem((spots, 8, 128), f32),
            vmem((spots, 8, 128), f32),
            vmem((spots, 128), f32),
            vmem((NZ, spots, 128), f32),
            vmem((spots, slots // spots, kept), bf16),
            vmem((spots, slots // spots, kept), bf16),
            vmem((NZ, slots // NZ, kept), bf16),
            vmem((NZ, slots // NZ, kept), bf16),
            vmem((slots, width), bf16),
            vmem((slots, width), bf16),
            vmem((TURNS, slots, 2 * PART), f32),
            vmem((TURNS, 2, HALF, PART), bf16),
            vmem((TURNS, 2, HALF, PART), bf16),
            vmem((TURNS, 2, slots, PART), bf16),
            vmem((TURNS, 2, slots, PART), bf16),
            vmem((TURNS, slots, 2 * PART), bf16),
            vmem((slots, PART), f32),
            vmem((slots, width), f32),
            vmem((8, slots), f32),
            vmem((NX - 1, 8, slots), f32),
            vmem((8, slots), f32),
            vmem((NX - 1, 8, slots), f32),
            dma((6,)),
            dma((GROUP,)),
            dma((GROUP,)),
            dma,
            dma,
            dma((spots,)),
            dma((NZ,)),
            dma((spots,)),
            dma((NZ,)),
            dma((4,)),
            dma((NX - 1,)),
            dma((NX - 1,)),
            dma((NX - 1,)),
            dma((NX - 1,)),
            dma((TURNS, 2)),
            dma((TURNS, 2)),
            dma((TURNS, 2)),
            dma((TURNS, 2)),
            dma((TURNS, 2, 2)),
            dma((TURNS, 2)),
        ],
        compiler_params=pltpu.CompilerParams(
            collective_id=0, has_side_effects=True, vmem_limit_bytes=59936 * 1024
        ),
    )(
        token_shard.reshape(1, tokens),
        token_row.reshape(1, tokens),
        kv_target,
        gain.reshape(1, width),
        key_value_weight,
        table,
    )


def solution(mesh):
    return jax.shard_map(
        on_device,
        mesh=mesh,
        in_specs=(
            P(("section", "wide"), None),
            P(("section", "wide")),
            P(("section", "wide"), "narrow"),
            P("narrow"),
            P(("section", "wide"), "narrow"),
            P(("section", "wide"), "narrow"),
        ),
        out_specs=P(("section", "wide"), "narrow"),
        check_vma=False,
    )
```

time: 418 us -> 92.9 us (0.22)
  the two profiles are of different devices: /device:TPU:1 before, /device:TPU:34 now
where the time goes in v2:
time: 92.9 us; the launch traced here: 92.7 us
  Pallas kernels  89.5 us (96%)
  local copies, waits for them, and re-layouts  3.16 us (3%)
    pallas_call x1, Pallas kernels, on_device(): pl.pallas_call(kernel, out_shape=jax.ShapeDtypeStruct(table.shape, bf16),...  89.5 us
    unnamed x1, local copies, waits for them, and re-layouts  3.16 us

profile of v2, /device:TPU:34, one launch (start us, length us, event | category | flops | bytes accessed | tf_op | source)
XLA Modules:
  0.0 92.7 jit_solution(859256165327242367)
XLA Ops:
  0.0 89.5 %shard_map.64 = bf16[512,2048]{1,0:T(8,128)(2,1)} custom-call(s32[1,128]{1,0:T(1,128)} %bitcast.4, s32[1,128]{1,0:T(1,128)} %bitcast.5, bf16[128,512]{1,0:T(8,128)(2,1)} %target_hbm.1, f32[1,2048]{1,0:T(1,128)} %bitcast.3, bf16[16,2048]{1,0:T(8,128)(2,1)} %weight_hbm.1, bf16[512,2048]{1,0:T(8,128)(2,1)} %table_hbm.1), custom_call_target="tpu_custom_call" | custom-call | tf_op jit(solution)/shard_map/pallas_call | solution.py:614
  89.5 3.2 %copy.8 = bf16[512,2048]{1,0:T(8,128)(2,1)} copy(bf16[512,2048]{1,0:T(8,128)(2,1)} %shard_map.64) | data formatting | bytes 4194304

commit v3 on v2

--- a/solution.py
+++ b/solution.py
@@ -15,6 +15,7 @@
 SPLIT = 512
 TILE = 256
 PART = 128
+DIRECT = (6, 7)
 HALF = 128
 TURNS = 8
 
@@ -26,7 +27,8 @@
     gain_hbm,
     weight_hbm,
     table_hbm,
-    out_ref,
+    grad_ref,
+    wanted_ref,
     shard,
     row,
     target,
@@ -48,6 +50,8 @@
     half_in,
     joint_out,
     joint_in,
+    direct_out,
+    direct_in,
     resid,
     inner,
     back,
@@ -75,6 +79,9 @@
     joint_sent,
     resid_recv,
     resid_sent,
+    direct_recv,
+    direct_sent,
+    across_sent,
 ):
     f32, bf16, i32 = jnp.float32, jnp.bfloat16, jnp.int32
     section, wide, x = lax.axis_index("section"), lax.axis_index("wide"), lax.axis_index("narrow")
@@ -276,30 +283,21 @@
     def send_goal(step):
         copy_goalz(zz_of(step), z).start()
 
-    def spread(distance):
-        first_hand(distance, -1, True)
-        first_hand(distance, 1, distance < NZ // 2 - 1)
-
-        @pl.when(distance <= 4)
-        def _():
-            for step in (11, 10):
-                send_goal(step - 2 * distance)
-                send_goal(2 * distance - step)
-
-        planes(distance - 1, -1, True)
-        planes(distance - 1, 1, True)
-        later(second_hand, distance - 1)
-        later(third_hand, distance - 2)
-
-    first_hand(1, -1, True)
-    first_hand(1, 1, True)
+    def both(hand, distance):
+        hand(distance, -1, True)
+        hand(distance, 1, True)
+
+    both(first_hand, 1)
+    for step in range(1, NY):
+        arrive("a", yy_of(step), z, c)
+        pass_on("a", yy_of(step), z, (after, before, partner))
+    both(first_hand, 2)
     each(1, spots, lambda step: copy_idy(here, around(step)).wait_recv())
     ids_all[...] = jnp.concatenate([ids_mid[spot][0:1, :] for spot in range(spots)], axis=0)
     each(1, NZ, lambda step: copy_idz(zz_of(step), z).start())
     ids_in[z] = ids_all[...]
-    for step in range(1, NY):
-        arrive("a", yy_of(step), z, c)
-        pass_on("a", yy_of(step), z, (after, before, partner))
+    both(planes, 1)
+    later(second_hand, 0)
 
     each(1, spots, lambda step: copy_goaly(here, around(step)).wait_recv())
     out_slot = lax.broadcasted_iota(i32, (slots, slots), 0)
@@ -309,11 +307,16 @@
     order = jnp.where(in_slot == from_slot, 1.0, 0.0).astype(bf16)
     arrived = goal_mid[...].reshape(slots, kept)
     goal_next[...] = jnp.dot(order, arrived, preferred_element_type=f32).astype(bf16).reshape(NZ, per_z, kept)
-    send_goal(NZ // 2)
+    for step in (8, 7, -7, 6, -6):
+        send_goal(step)
     goal[z] = goal_next[z]
 
-    second_hand(0, -1)
-    each(2, 3, spread)
+    both(first_hand, 3)
+    both(planes, 2)
+    later(second_hand, 1)
+    later(third_hand, 0)
+    for step in (5, -5, 4, -4):
+        send_goal(step)
 
     each(1, NZ, lambda step: copy_idz(z, zz_of(step)).wait_recv())
     loads[5].wait()
@@ -360,7 +363,8 @@
     for step in range(1, NX):
         copy_square(step).start()
 
-    each(3, 4, spread)
+    later(second_hand, 2)
+    later(third_hand, 1)
 
     for step in range(1, NX):
         copy_square(step).wait_recv()
@@ -379,6 +383,16 @@
     ]
     blocks = PART // depth
     right, left = xx_of(1), xx_of(-1)
+
+    def copy_direct(turn):
+        at = turn - DIRECT[0]
+        return remote(direct_out.at[at], direct_in.at[at], direct_sent.at[at], direct_recv.at[at], beside(xx_of(2)))
+
+    def copy_resid_across(turn, part):
+        piece = resid.at[turn, :, part_cols(part)]
+        return remote(
+            piece, piece, across_sent.at[turn - DIRECT[0]], resid_recv.at[turn, part, 0], beside(xx_of(2))
+        )
 
     def tile_rows(part, pair):
         return pl.ds((part * pairs + pair) * blocks, blocks)
@@ -433,6 +447,21 @@
         rows = jnp.concatenate([full[tile_rows(part, pair)].reshape(PART, width) for part in order], axis=0)
         partial[turn] = lax.dot_general(normed[...], rows, (((1,), (1,)), ((), ())), preferred_element_type=f32)
 
+        if turn in DIRECT:
+
+            @pl.when(dest)
+            def _():
+                direct_out[turn - DIRECT[0]] = partial[turn, :, 0:PART].astype(bf16)
+                copy_direct(turn).start()
+
+            @pl.when(jnp.logical_not(dest))
+            def _():
+                for side in range(2):
+                    joint_out[turn, side] = partial[turn, :, side * PART : (side + 1) * PART].astype(bf16)
+                    copy_joint(turn, side).start()
+
+            return
+
         @pl.when(dest)
         def _():
             for side in range(2):
@@ -457,24 +486,34 @@
             for side in range(2):
                 copy_joint(turn, side).wait_recv()
             projected = partial[turn, :, PART:] + joint_in[turn, 0].astype(f32) + joint_in[turn, 1].astype(f32)
+            if turn in DIRECT:
+                copy_direct(turn).wait_recv()
+                projected += direct_in[turn - DIRECT[0]].astype(f32)
             wished = goal[:, :, part_cols(pair % (pairs // 2))].reshape(slots, PART)
             residual = (projected - wished.astype(f32)).astype(bf16)
             resid[turn, :, part_cols(x // 2)] = residual
             for side in range(2):
                 copy_resid(turn, x // 2, side).start()
+            if turn in DIRECT:
+                copy_resid_across(turn, x // 2).start()
             inner[...] += projected * residual.astype(f32)
 
     def relay_resid(turn):
         @pl.when(jnp.logical_not(ends_here(pair_at[turn])))
         def _():
             copy_resid(turn, left // 2, 0).wait_recv()
-            copy_resid_half(turn, left // 2, 0).start()
+            if turn not in DIRECT:
+                copy_resid_half(turn, left // 2, 0).start()
             copy_resid(turn, right // 2, 1).wait_recv()
-            copy_resid_half(turn, right // 2, 1).start()
+            if turn not in DIRECT:
+                copy_resid_half(turn, right // 2, 1).start()
 
     def await_resid(turn):
         @pl.when(ends_here(pair_at[turn]))
         def _():
+            if turn in DIRECT:
+                copy_resid_across(turn, 1 - x // 2).wait_recv()
+                return
             for side in range(2):
                 copy_resid_half(turn, 1 - x // 2, side).wait_recv()
 
@@ -538,12 +577,10 @@
             each(1, NZ, lambda step: copy_goalz(z, zz_of(step)).wait_recv())
         work(jobs[distance][3])
     project(7)
-    relay_sums(6)
     subtract(5)
     relay_resid(4)
+    subtract(6)
     accumulate((0, 1))
-    relay_sums(7)
-    subtract(6)
     relay_resid(5)
     subtract(7)
 
@@ -551,11 +588,11 @@
     inner_out[...] = jnp.broadcast_to(inner_row, inner_out.shape)
     for step in range(1, NX):
         copy_inner(step).start()
+    accumulate((2, 3, 4, 5))
     relay_resid(6)
-    accumulate((2, 3, 4, 5))
     relay_resid(7)
     wanted_row = as_row(wanted)
-    put = jnp.where(lax.broadcasted_iota(i32, (rows_here, slots), 0).astype(f32) == wanted_row, 1.0, 0.0).astype(bf16)
+    wanted_ref[...] = jnp.broadcast_to(wanted_row, wanted_ref.shape)
     for step in range(1, NX):
         copy_inner(step).wait_recv()
     inner_all = inner_row
@@ -568,8 +605,7 @@
     def finish(tile):
         at = pl.ds(pl.multiple_of(tile * TILE, TILE), TILE)
         weighted = (back[:, at] + step_back(6, at) + step_back(7, at)) * gain[:, at]
-        grad = (row_scale * weighted - hidden[:, at].astype(f32) * pull).astype(bf16)
-        out_ref[:, at] = jnp.dot(put, grad, preferred_element_type=f32).astype(bf16)
+        grad_ref[:, at] = (row_scale * weighted - hidden[:, at].astype(f32) * pull).astype(bf16)
 
     each(0, width // TILE, finish)
 
@@ -590,16 +626,28 @@
 
         @pl.when(dest)
         def _():
+            if turn in DIRECT:
+                copy_direct(turn).wait_send()
+                copy_resid_across(turn, x // 2).wait_send()
             for side in range(2):
-                copy_half(turn, side).wait_send()
+                if turn not in DIRECT:
+                    copy_half(turn, side).wait_send()
                 copy_resid(turn, x // 2, side).wait_send()
 
         @pl.when(jnp.logical_not(dest))
         def _():
-            copy_resid_half(turn, left // 2, 0).wait_send()
-            copy_resid_half(turn, right // 2, 1).wait_send()
+            if turn not in DIRECT:
+                copy_resid_half(turn, left // 2, 0).wait_send()
+                copy_resid_half(turn, right // 2, 1).wait_send()
             for side in range(2):
                 copy_joint(turn, side).wait_send()
+
+
+def put_rows(wanted_ref, grad_ref, out_ref):
+    rows = out_ref.shape[0]
+    at = lax.broadcasted_iota(jnp.int32, (rows, grad_ref.shape[0]), 0).astype(jnp.float32)
+    put = jnp.where(at == wanted_ref[0:1, :], 1.0, 0.0).astype(jnp.bfloat16)
+    out_ref[...] = jnp.dot(put, grad_ref[...], preferred_element_type=jnp.float32).astype(out_ref.dtype)
 
 
 def on_device(token_shard, token_row, table, gain, key_value_weight, kv_target):
@@ -611,11 +659,11 @@
     bf16, f32, i32 = jnp.bfloat16, jnp.float32, jnp.int32
     dma, vmem = pltpu.SemaphoreType.DMA, pltpu.VMEM
     outside = pl.BlockSpec(memory_space=pltpu.HBM)
-    return pl.pallas_call(
+    grad, wanted = pl.pallas_call(
         kernel,
-        out_shape=jax.ShapeDtypeStruct(table.shape, bf16),
+        out_shape=(jax.ShapeDtypeStruct((slots, width), bf16), jax.ShapeDtypeStruct((8, slots), f32)),
         in_specs=[outside] * 6,
-        out_specs=pl.BlockSpec(memory_space=vmem),
+        out_specs=(pl.BlockSpec(memory_space=vmem),) * 2,
         scratch_shapes=[
             vmem((1, tokens), i32),
             vmem((1, tokens), i32),
@@ -638,6 +686,8 @@
             vmem((TURNS, 2, HALF, PART), bf16),
             vmem((TURNS, 2, slots, PART), bf16),
             vmem((TURNS, 2, slots, PART), bf16),
+            vmem((len(DIRECT), slots, PART), bf16),
+            vmem((len(DIRECT), slots, PART), bf16),
             vmem((TURNS, slots, 2 * PART), bf16),
             vmem((slots, PART), f32),
             vmem((slots, width), f32),
@@ -665,6 +715,9 @@
             dma((TURNS, 2)),
             dma((TURNS, 2, 2)),
             dma((TURNS, 2)),
+            dma((len(DIRECT),)),
+            dma((len(DIRECT),)),
+            dma((len(DIRECT),)),
         ],
         compiler_params=pltpu.CompilerParams(
             collective_id=0, has_side_effects=True, vmem_limit_bytes=59936 * 1024
@@ -677,6 +730,17 @@
         key_value_weight,
         table,
     )
+    step = width // 2
+    return pl.pallas_call(
+        put_rows,
+        out_shape=jax.ShapeDtypeStruct(table.shape, bf16),
+        grid=(width // step,),
+        in_specs=[
+            pl.BlockSpec((8, slots), lambda tile: (0, 0)),
+            pl.BlockSpec((slots, step), lambda tile: (0, tile)),
+        ],
+        out_specs=pl.BlockSpec((table.shape[0], step), lambda tile: (0, tile)),
+    )(wanted, grad)
 
 
 def solution(mesh):

time: 92.9 us -> 89.1 us (0.959)
  the two profiles are of different devices: /device:TPU:34 before, /device:TPU:33 now
where the time goes in v3:
time: 89.1 us; the launch traced here: 88.9 us
  Pallas kernels  88.9 us (100%)
    pallas_call x1, Pallas kernels, on_device(): pl.pallas_call(kernel, out_shape=(jax.ShapeDtypeStruct((slots, width), bf...  86 us
    pallas_call x1, Pallas kernels, on_device(): pl.pallas_call(put_rows, out_shape=jax.ShapeDtypeStruct(table.shape, bf16...  2.95 us

profile of v3, /device:TPU:33, one launch (start us, length us, event | category | flops | bytes accessed | tf_op | source)
XLA Modules:
  0.0 88.9 jit_solution(12390225128207340872)
XLA Ops:
  0.0 86.0 %shard_map.64 = (bf16[256,2048]{1,0:T(8,128)(2,1)}, f32[8,256]{1,0:T(8,128)}) custom-call(s32[1,128]{1,0:T(1,128)} %bitcast.4, s32[1,128]{1,0:T(1,128)} %bitcast.5, bf16[128,512]{1,0:T(8,128)(2,1)} %target_hbm.1, f32[1,2048]{1,0:T(1,128)} %bitcast.3, bf16[16,2048]{1,0:T(8,128)(2,1)} %weight_hbm.1, bf16[512,2048]{1,0:T(8,128)(2,1)} %table_hbm.1), custom_call_target="tpu_custom_call" | custom-call | tf_op jit(solution)/shard_map/pallas_call | solution.py:662
  86.0 2.9 %shard_map.65 = bf16[512,2048]{1,0:T(8,128)(2,1)} custom-call(f32[8,256]{1,0:T(8,128)} %get-tuple-element.7.wanted_ref, bf16[256,2048]{1,0:T(8,128)(2,1)} %get-tuple-element.8.grad_ref), custom_call_target="tpu_custom_call" | custom-call | tf_op jit(solution)/shard_map/pallas_call | solution.py:734

commit v4 on v3

--- a/solution.py
+++ b/solution.py
@@ -82,6 +82,7 @@
     direct_recv,
     direct_sent,
     across_sent,
+    entered,
 ):
     f32, bf16, i32 = jnp.float32, jnp.bfloat16, jnp.int32
     section, wide, x = lax.axis_index("section"), lax.axis_index("wide"), lax.axis_index("narrow")
@@ -137,11 +138,8 @@
 
     barrier = pltpu.get_barrier_semaphore()
 
-    def greet_z(step, carry):
+    for step in (1, -1):
         pl.semaphore_signal(barrier, inc=1, device_id=device(y, zz_of(step), c, x), device_id_type=MESH)
-        return carry
-
-    lax.fori_loop(1, NZ, greet_z, 0)
 
     def greet_y(step, carry):
         other = lax.rem(here + step, spots)
@@ -178,7 +176,22 @@
     )
     loads[2].wait()
 
-    pl.semaphore_wait(barrier, (NZ - 1) + (spots - 1) + (NX - 1))
+    pl.semaphore_wait(barrier, 2 + (spots - 1) + (NX - 1))
+
+    def tell(side, distance):
+        to = device(y, zz_of(-1 if side else 1), c, x)
+        pl.semaphore_signal(entered.at[side, distance], inc=1, device_id=to, device_id_type=MESH)
+
+    def learn(distance):
+        for side in range(2):
+            last = NZ // 2 - side
+            if distance <= last:
+                pl.semaphore_wait(entered.at[side, distance], 1)
+                if distance < last:
+                    tell(side, distance + 1)
+
+    tell(0, 2)
+    tell(1, 2)
 
     def spot_device(spot):
         return device(spot // 2, z, spot % 2, x)
@@ -287,11 +300,18 @@
         hand(distance, -1, True)
         hand(distance, 1, True)
 
+    learn(2)
+    learn(3)
     both(first_hand, 1)
+    learn(4)
+    learn(5)
     for step in range(1, NY):
         arrive("a", yy_of(step), z, c)
         pass_on("a", yy_of(step), z, (after, before, partner))
+    learn(6)
     both(first_hand, 2)
+    learn(7)
+    learn(8)
     each(1, spots, lambda step: copy_idy(here, around(step)).wait_recv())
     ids_all[...] = jnp.concatenate([ids_mid[spot][0:1, :] for spot in range(spots)], axis=0)
     each(1, NZ, lambda step: copy_idz(zz_of(step), z).start())
@@ -307,16 +327,15 @@
     order = jnp.where(in_slot == from_slot, 1.0, 0.0).astype(bf16)
     arrived = goal_mid[...].reshape(slots, kept)
     goal_next[...] = jnp.dot(order, arrived, preferred_element_type=f32).astype(bf16).reshape(NZ, per_z, kept)
-    for step in (8, 7, -7, 6, -6):
+    send_goal(8)
+    goal[z] = goal_next[z]
+
+    both(first_hand, 3)
+    for step in (7, -7, 1, -1):
         send_goal(step)
-    goal[z] = goal_next[z]
-
-    both(first_hand, 3)
     both(planes, 2)
     later(second_hand, 1)
     later(third_hand, 0)
-    for step in (5, -5, 4, -4):
-        send_goal(step)
 
     each(1, NZ, lambda step: copy_idz(z, zz_of(step)).wait_recv())
     loads[5].wait()
@@ -537,13 +556,17 @@
         each(0, width // TILE, add)
 
     inner[...] = jnp.zeros(inner.shape, f32)
+    def relay_both(turn):
+        relay_resid(turn)
+        relay_resid(turn + 1)
+
     far = NZ // 2
     jobs = {
         4: ((project, 0), None, None, None),
         5: ((project, 1), (relay_sums, 0), None, None),
-        6: ((project, 2), (relay_sums, 1), None, (subtract, 0)),
-        7: ((project, 3), (relay_sums, 2), (subtract, 1), (relay_resid, 0)),
-        8: ((project, 4), (relay_sums, 3), (subtract, 2), (relay_resid, 1)),
+        6: ((project, 2), (relay_sums, 1), None, None),
+        7: ((project, 3), (relay_sums, 2), (subtract, 0), (subtract, 1)),
+        8: ((project, 4), (relay_sums, 3), (subtract, 2), (relay_both, 0)),
         9: ((project, 5), (relay_sums, 4), (subtract, 3), (relay_resid, 2)),
         10: ((project, 6), (relay_sums, 5), (subtract, 4), (relay_resid, 3)),
     }
@@ -557,12 +580,8 @@
             first_hand(distance, -1, distance < far)
             if distance < far:
                 first_hand(distance, 1, distance < far - 1)
-        if distance == 4:
-            for step in (3, -3, 2, -2):
-                send_goal(step)
-        if distance == 5:
-            for step in (1, -1):
-                send_goal(step)
+        for step in {4: (6, -6, 2, -2), 5: (5, -5, 3, -3), 6: (4, -4)}.get(distance, ()):
+            send_goal(step)
         work(jobs[distance][0])
         if distance - 1 <= far:
             planes(distance - 1, -1, distance - 1 < far)
@@ -571,10 +590,10 @@
         work(jobs[distance][1])
         if distance - 1 <= far:
             later(second_hand, distance - 1)
+        if distance == 7:
+            each(1, NZ, lambda step: copy_goalz(z, zz_of(step)).wait_recv())
         work(jobs[distance][2])
         later(third_hand, distance - 2)
-        if distance == 6:
-            each(1, NZ, lambda step: copy_goalz(z, zz_of(step)).wait_recv())
         work(jobs[distance][3])
     project(7)
     subtract(5)
@@ -718,6 +737,7 @@
             dma((len(DIRECT),)),
             dma((len(DIRECT),)),
             dma((len(DIRECT),)),
+            pltpu.SemaphoreType.REGULAR((2, NZ // 2 + 1)),
         ],
         compiler_params=pltpu.CompilerParams(
             collective_id=0, has_side_effects=True, vmem_limit_bytes=59936 * 1024

time: 89.1 us -> 87 us (0.976)
  Pallas kernels: 88.9 us -> 86.8 us
    pallas_call x1, Pallas kernels: 86 us -> 83.9 us  [on_device(): pl.pallas_call(kernel, out_shape=(jax.ShapeDtypeStruct((slots, width), bf...]
where the time goes in v4:
time: 87 us; the launch traced here: 86.8 us
  Pallas kernels  86.8 us (100%)
    pallas_call x1, Pallas kernels, on_device(): pl.pallas_call(kernel, out_shape=(jax.ShapeDtypeStruct((slots, width), bf...  83.9 us
    pallas_call x1, Pallas kernels, on_device(): pl.pallas_call(put_rows, out_shape=jax.ShapeDtypeStruct(table.shape, bf16...  2.95 us

profile of v4, /device:TPU:33, one launch (start us, length us, event | category | flops | bytes accessed | tf_op | source)
XLA Modules:
  0.0 86.8 jit_solution(5520073919182848924)
XLA Ops:
  0.0 83.9 %shard_map.64 = (bf16[256,2048]{1,0:T(8,128)(2,1)}, f32[8,256]{1,0:T(8,128)}) custom-call(s32[1,128]{1,0:T(1,128)} %bitcast.4, s32[1,128]{1,0:T(1,128)} %bitcast.5, bf16[128,512]{1,0:T(8,128)(2,1)} %target_hbm.1, f32[1,2048]{1,0:T(1,128)} %bitcast.3, bf16[16,2048]{1,0:T(8,128)(2,1)} %weight_hbm.1, bf16[512,2048]{1,0:T(8,128)(2,1)} %table_hbm.1), custom_call_target="tpu_custom_call" | custom-call | tf_op jit(solution)/shard_map/pallas_call | solution.py:681
  83.9 3.0 %shard_map.65 = bf16[512,2048]{1,0:T(8,128)(2,1)} custom-call(f32[8,256]{1,0:T(8,128)} %get-tuple-element.7.wanted_ref, bf16[256,2048]{1,0:T(8,128)(2,1)} %get-tuple-element.8.grad_ref), custom_call_target="tpu_custom_call" | custom-call | tf_op jit(solution)/shard_map/pallas_call | solution.py:754
